TPU v7x, 32 devices: a whole 2x2x4 slice. The times are simulated.
32 devices in a mesh: feat: 16 (over z, y, x), dp: 2 (over core).
Axes of the slice: x: 2, y: 2, z: 4, core: 2. Of those that a mesh axis runs over, the one named last changes fastest.
Arguments:
- activations: bfloat16 [1024, 16384], P('dp', 'feat')
- norm_gain: float32 [16384], replicated, may hold values from 0.5 to 1.5
- weights: float32 [1024, 16384], P('dp', 'feat'), may hold values from -6 to 6
- inverse_factor: float32 [128, 16384], P(None, 'feat'), as said below
- grid_scales: float32 [1024], P('dp'), may hold values from 0.5 to 2
Outputs:
- hessian: float32 [16384, 16384], P('dp', 'feat')
- updated_weights: float32 [1024, 16384], P('dp', 'feat')
Inputs may be any that keep to these rules, and one draw needn't show every extreme that they name: `inverse_factor`: in the first 128 columns, the diagonal lies in 1 to 2 and entries below it are zero.
All inputs are finite; a program needn't handle non-finite values.
Results may differ from a plain program's by a relative error of at most 0.012.
Values may be sent and summed in bfloat16 or wider, within the bound.
No kernel may reach another device: no remote copies, remote signals or barrier semaphores. Data moves between devices by JAX's collectives and lax.ppermute only.
A program may use at most 128 MiB of HBM per device.

v0:
```python
import math
import jax
import jax.numpy as jnp
from jax import lax
from jax.sharding import PartitionSpec as P

norm_epsilon = 1e-05
full_turn = 2.0 * math.pi


def spread(value, axis, source):
    kept = jnp.where(lax.axis_index(axis) == source, value, 0).astype(value.dtype)
    return lax.psum(kept, axis)


def quantize_panel(panel_rows, factor_block, grid_scales):
    panel_width = factor_block.shape[0]
    diagonal_entries = jnp.diagonal(factor_block)
    positions = jnp.arange(panel_width)

    def advance(index, carry):
        working, quantized, residue = carry
        current = lax.dynamic_index_in_dim(working, index, 0, keepdims=False)
        grid_ratio = current / grid_scales
        dequantized = grid_scales * (grid_ratio - jnp.sin(full_turn * grid_ratio) / full_turn)
        pivot_entry = lax.dynamic_index_in_dim(diagonal_entries, index, 0, keepdims=False)
        scaled_error = (current - dequantized) / pivot_entry
        factor_row = lax.dynamic_index_in_dim(factor_block, index, 0, keepdims=False)
        factor_row = jnp.where(positions > index, factor_row, jnp.zeros_like(factor_row))
        working = working - factor_row[:, None] * scaled_error[None, :]
        quantized = lax.dynamic_update_index_in_dim(quantized, dequantized, index, 0)
        residue = lax.dynamic_update_index_in_dim(residue, scaled_error, index, 0)
        return (working, quantized, residue)

    blank = jnp.zeros_like(panel_rows)
    final = lax.fori_loop(0, panel_width, advance, (panel_rows, blank, blank))
    return (final[1], final[2])


def body(activations, norm_gain, weights, inverse_factor, grid_scales):
    shard_width = activations.shape[1]
    row_count = activations.shape[0]
    full_width = shard_width * lax.axis_size("feat")
    token_total = row_count * lax.axis_size("dp")
    own_start = lax.axis_index("feat") * shard_width
    own_gain = lax.dynamic_slice_in_dim(norm_gain, own_start, shard_width, 0)
    widened = activations.astype(jnp.float32)
    own_squares = jnp.sum(widened * widened, axis=1, keepdims=True)
    row_squares = lax.psum(own_squares, "feat")
    normed = (
        widened * lax.rsqrt(row_squares / full_width + norm_epsilon) * own_gain[None, :]
    ).astype(jnp.bfloat16)
    gathered = lax.all_gather(normed, "feat", axis=1, tiled=True)
    product = lax.dot_general(
        gathered, normed, (((0,), (0,)), ((), ())), preferred_element_type=jnp.float32
    )
    hessian = lax.psum_scatter(
        (product / token_total).astype(jnp.bfloat16), "dp", scatter_dimension=0, tiled=True
    ).astype(jnp.float32)
    panel_width = inverse_factor.shape[0]
    quantized, residue = quantize_panel(
        weights[:, :panel_width].T, inverse_factor[:, :panel_width], grid_scales
    )
    residue = spread(residue.astype(jnp.bfloat16), "feat", 0).astype(residue.dtype)
    shift_terms = lax.dot_general(
        residue,
        inverse_factor,
        (((0,), (0,)), ((), ())),
        precision=lax.Precision.HIGHEST,
        preferred_element_type=jnp.float32,
    )
    updated = weights - shift_terms
    column_ids = lax.broadcasted_iota(jnp.int32, weights.shape, 1)
    panel_mask = (column_ids < panel_width) & (lax.axis_index("feat") == 0)
    padded_panel = jnp.pad(quantized.T, ((0, 0), (0, shard_width - panel_width)))
    updated = jnp.where(panel_mask, padded_panel, updated)
    return (hessian, updated)


def solution(mesh):
    placed = (P("dp", "feat"), P(), P("dp", "feat"), P(None, "feat"), P("dp"))
    return jax.shard_map(
        body,
        mesh=mesh,
        in_specs=placed,
        out_specs=(P("dp", "feat"), P("dp", "feat")),
        check_vma=False,
    )
```

profile of v0, /device:TPU:0, one launch (start us, length us, event | category | flops | bytes accessed | tf_op | source)
XLA Modules:
  0.0 446.7 jit_solution(7831855614738528062)
XLA Ops:
  7.2 1.6 fusion.2
  8.8 43.6 %psum.14 = f32[512,1]{0,1:T(1,128)S(1)} all-reduce(f32[512,1]{0,1:T(1,128)S(1)} %bitcast.28), channel_id=1, replica_groups=mesh['feat'=16,'dp'=2] {'feat'}, use_global_device_ids=true, to_apply=%region_1.0 | all-reduce | flops 512 | bytes 4096 | tf_op jit(solution)/shard_map/psum | solution.py:49
  53.2 2.5 fusion.4
  56.0 1.2 gather_fusion
  57.2 217.8 %while.18 = (s32[]{:T(128)}, f32[128,512]{1,0:T(8,128)S(1)}, f32[128,512]{1,0:T(8,128)S(1)}, bf16[128,512]{1,0:T(8,128)(2,1)S(1)}, f32[128,128]{1,0:T(8,128)S(1)...) while((s32[]{:T(128)}, f32[128,512]{1,0:T(8,128)S(1)}, ...), condition=%wide.region_4.5_spmd.clone, body=%wide.region_3.4_spmd.clone.sunk | while | flops 134914 | bytes 545401 | solution.py:36
  57.9 0.8 subtract_divide_fusion.2
  59.6 0.8 subtract_divide_fusion.2
  63.0 0.8 subtract_divide_fusion.2
  64.7 0.8 subtract_divide_fusion.2
  66.4 0.8 subtract_divide_fusion.2
  68.1 0.8 subtract_divide_fusion.2
  69.8 0.8 subtract_divide_fusion.2
  71.5 0.8 subtract_divide_fusion.2
  80.0 0.8 subtract_divide_fusion.2
  81.7 0.8 subtract_divide_fusion.2
  88.5 0.8 subtract_divide_fusion.2
  105.6 0.8 subtract_divide_fusion.2
  107.3 0.8 subtract_divide_fusion.2
  109.0 0.8 subtract_divide_fusion.2
  110.7 0.8 subtract_divide_fusion.2
  112.4 0.8 subtract_divide_fusion.2
  114.1 0.8 subtract_divide_fusion.2
  137.9 0.8 subtract_divide_fusion.2
  139.6 0.8 subtract_divide_fusion.2
  141.3 0.8 subtract_divide_fusion.2
  143.0 0.8 subtract_divide_fusion.2
  146.4 0.8 subtract_divide_fusion.2
  158.3 0.8 subtract_divide_fusion.2
  160.0 0.8 subtract_divide_fusion.2
  161.7 0.8 subtract_divide_fusion.2
  163.4 0.8 subtract_divide_fusion.2
  165.1 0.8 subtract_divide_fusion.2
  166.8 0.8 subtract_divide_fusion.2
  168.5 0.8 subtract_divide_fusion.2
  170.2 0.8 subtract_divide_fusion.2
  180.4 0.8 subtract_divide_fusion.2
  199.1 0.8 subtract_divide_fusion.2
  200.8 0.8 subtract_divide_fusion.2
  202.5 0.8 subtract_divide_fusion.2
  204.2 0.8 subtract_divide_fusion.2
  205.9 0.8 subtract_divide_fusion.2
  207.6 0.8 subtract_divide_fusion.2
  231.5 0.8 subtract_divide_fusion.2
  275.8 27.8 %multiply_convert_fusion = bf16[16384,1024]{1,0:T(8,128)(2,1)} fusion(bf16[512,16384]{1,0:T(8,128)(2,1)} %all-gather.2.cloned.1.call-done, bf16[512,1024]{1,0:T(8,128)(2,1)S(1)} %copy-done), kind=kOutput, calls=%fused_computation.6 | convolution fusion | flops 17213423616 | bytes 51380224 | tf_op jit(solution)/shard_map/dot_general | solution.py:54
  303.8 73.4 %all-reduce.3.cloned.1.call-done = bf16[128,512]{1,0:T(8,128)(2,1)} async-done(((bf16[128,512]{1,0:T(8,128)(2,1)}), bf16[128,512]{1,0:T(8,128)(2,1)}) %all-reduce.3.cloned.1.call-update) | async-done | bytes 131088 | tf_op jit(solution)/shard_map/psum | solution.py:13
  377.2 3.3 subtract_select_fusion
  380.5 41.1 %reduce-scatter.2.cloned.1.call-done = bf16[8192,1024]{1,0:T(8,128)(2,1)} async-done(((bf16[16384,1024]{1,0:T(8,128)(2,1)}), bf16[8192,1024]{1,0:T(8,128)(2,1)}) %reduce-scatter.2.cloned.1.call-update) | async-done | bytes 16777232 | tf_op jit(solution)/shard_map/reduce_scatter | solution.py:57
  421.6 18.6 %convert_element_type.23 = f32[8192,1024]{1,0:T(8,128)} convert(bf16[8192,1024]{1,0:T(8,128)(2,1)} %reduce-scatter.2.cloned.1.call-done) | non-fusion elementwise | flops 8388608 | bytes 50331648 | tf_op jit(solution)/shard_map/convert_element_type | solution.py:59
  (757 shorter events, 184.4 us)
Async XLA Ops:
  7.2 268.6 %all-gather.2.cloned.1.call-start = ((), (), s32[]{:S(2)}) async-start(), calls=%async_computation.1 | async-start | bytes 17825792 | tf_op jit(solution)/shard_map/all_gather | solution.py:53
  7.2 48.6 %copy-start.2 = (f32[128,1024]{1,0:T(8,128)S(1)}, f32[128,1024]{1,0:T(8,128)}, u32[]{:S(2)}) copy-start(f32[128,1024]{1,0:T(8,128)} %param.10) | copy-start | bytes 1572868
  8.8 47.0 %slice-start = ((f32[512,1024]{1,0:T(8,128)}), f32[512,128]{1,0:T(8,128)S(1)}, s32[]{:S(2)}) async-start(f32[512,1024]{1,0:T(8,128)} %param.9), calls=%async_computation.4 | async-start | bytes 524288 | tf_op jit(solution)/shard_map/slice | solution.py:62
  53.1 4.1 copy-start.3
  55.7 321.5 %all-reduce.3.cloned.1.call-start = ((), (), s32[]{:S(2)}) async-start(), calls=%async_computation.3 | async-start | bytes 262144 | tf_op jit(solution)/shard_map/psum | solution.py:13
  55.9 219.9 %copy-start = (bf16[512,1024]{1,0:T(8,128)(2,1)S(1)}, bf16[512,1024]{1,0:T(8,128)(2,1)}, u32[]{:S(2)}) copy-start(bf16[512,1024]{1,0:T(8,128)(2,1)} %fusion.4) | copy-start | bytes 3145732
  275.7 145.8 %reduce-scatter.2.cloned.1.call-start = ((), (), s32[]{:S(2)}) async-start(), calls=%async_computation.2 | async-start | bytes 50331648 | tf_op jit(solution)/shard_map/reduce_scatter | solution.py:57
  303.6 73.6 %copy-start.1 = (f32[512,1024]{1,0:T(8,128)S(1)}, f32[512,1024]{1,0:T(8,128)}, u32[]{:S(2)}) copy-start(f32[512,1024]{1,0:T(8,128)} %param.9) | copy-start | bytes 6291460
Sparse Core Ops, SparseCore 0:
  55.8 191.9 all-gather.1
  275.9 101.2 all-reduce.2
  380.0 41.4 reduce-scatter.1
where the time goes:
time: 448 us; the launch traced here: 447 us
  other arithmetic  137 us (31%)
  waiting for transfers between devices  115 us (26%)
  local copies, waits for them, and re-layouts  101 us (23%)
  blocking collectives  43.6 us (10%)
  matrix products  31.1 us (7%)
  between operations  13.9 us (3%)
  loops' own time  5.98 us (1%)
    div x128, other arithmetic, advance(): scaled_error = (current - dequantized) / pivot_entry  98.6 us
    dynamic_slice x128, local copies, waits for them, and re-layouts, advance(): lax.dynamic_index_in_dim(diagonal_entries, index, 0, keepdims=False)  85 us
    psum x1, waiting for transfers between devices, spread(): return lax.psum(kept, axis)  73.4 us
    psum x1, blocking collectives, body(): row_squares = lax.psum(own_squares, 'feat')  43.6 us
    reduce_scatter x1, waiting for transfers between devices, body(): lax.psum_scatter((product / token_total).astype(jnp.bfloat16), 'dp', scat...  41.1 us
    dot_general x1, matrix products, body(): lax.dot_general(gathered, normed, (((0,), (0,)), ((), ())), preferred_ele...  27.8 us
    convert_element_type x1, other arithmetic, body(): hessian = lax.psum_scatter((product / token_total).astype(jnp.bfloat16),...  18.6 us
    sub x128, other arithmetic, advance(): working = working - factor_row[:, None] * scaled_error[None, :]  12.9 us
  transfers between devices with their start and end apart: 3, of which 2 were waited for; matrix products, arithmetic and copies ran while one was open for 55% of the time, Pallas kernels for 0%

commit v1 on v0

--- a/solution.py
+++ b/solution.py
@@ -1,3 +1,4 @@
+import functools
 import math
 import jax
 import jax.numpy as jnp
@@ -6,6 +7,14 @@
 
 norm_epsilon = 1e-05
 full_turn = 2.0 * math.pi
+
+
+def move_sample(patch, bus_axis):
+    near = jax.lax.all_gather(patch, bus_axis).sum(axis=0)
+    return near
+
+
+watch_the_rings = functools.partial(move_sample, bus_axis="feat")
 
 
 def spread(value, axis, source):
@@ -46,7 +55,7 @@
     own_gain = lax.dynamic_slice_in_dim(norm_gain, own_start, shard_width, 0)
     widened = activations.astype(jnp.float32)
     own_squares = jnp.sum(widened * widened, axis=1, keepdims=True)
-    row_squares = lax.psum(own_squares, "feat")
+    row_squares = watch_the_rings(own_squares)
     normed = (
         widened * lax.rsqrt(row_squares / full_width + norm_epsilon) * own_gain[None, :]
     ).astype(jnp.bfloat16)

time: 448 us -> 447 us (level)
    psum x1 -> x0, blocking collectives: 43.6 us -> none  [body(): row_squares = lax.psum(own_squares, 'feat')]
    all_gather x0 -> x1, blocking collectives: none -> 42.7 us  [move_sample(): near = jax.lax.all_gather(patch, bus_axis).sum(axis=0)]
where the time goes in v1:
time: 447 us; the launch traced here: 446 us
  other arithmetic  137 us (31%)
  waiting for transfers between devices  115 us (26%)
  local copies, waits for them, and re-layouts  101 us (23%)
  blocking collectives  42.7 us (10%)
  matrix products  31.1 us (7%)
  between operations  13.9 us (3%)
  loops' own time  5.98 us (1%)
    div x128, other arithmetic, advance(): scaled_error = (current - dequantized) / pivot_entry  98.6 us
    dynamic_slice x128, local copies, waits for them, and re-layouts, advance(): lax.dynamic_index_in_dim(diagonal_entries, index, 0, keepdims=False)  85 us
    psum x1, waiting for transfers between devices, spread(): return lax.psum(kept, axis)  73.4 us
    all_gather x1, blocking collectives, move_sample(): near = jax.lax.all_gather(patch, bus_axis).sum(axis=0)  42.7 us
    reduce_scatter x1, waiting for transfers between devices, body(): lax.psum_scatter((product / token_total).astype(jnp.bfloat16), 'dp', scat...  41.1 us
    dot_general x1, matrix products, body(): lax.dot_general(gathered, normed, (((0,), (0,)), ((), ())), preferred_ele...  27.7 us
    convert_element_type x1, other arithmetic, body(): hessian = lax.psum_scatter((product / token_total).astype(jnp.bfloat16),...  18.6 us
    sub x128, other arithmetic, advance(): working = working - factor_row[:, None] * scaled_error[None, :]  12.9 us
  transfers between devices with their start and end apart: 3, of which 2 were waited for; matrix products, arithmetic and copies ran while one was open for 55% of the time, Pallas kernels for 0%

profile of v1, /device:TPU:0, one launch (start us, length us, event | category | flops | bytes accessed | tf_op | source)
XLA Modules:
  0.0 445.8 jit_solution(2222960148220124596)
XLA Ops:
  7.2 1.6 fusion.2
  8.8 42.7 %all-gather.1 = f32[16,1,512]{2,1,0:T(1,128)S(1)} all-gather(f32[1,1,512]{2,1,0:T(1,128)S(1)} %bitcast.26), channel_id=2, replica_groups=mesh['feat'=16,'dp'=2] {'feat'}, dimensions={0}, use_global_device_ids=true | all-gather | bytes 34816 | tf_op jit(solution)/shard_map/all_gather | solution.py:13
  52.2 2.5 fusion.4
  55.1 1.2 gather_fusion
  56.3 217.8 %while.18 = (s32[]{:T(128)}, f32[128,512]{1,0:T(8,128)S(1)}, f32[128,512]{1,0:T(8,128)S(1)}, bf16[128,512]{1,0:T(8,128)(2,1)S(1)}, f32[128,128]{1,0:T(8,128)S(1)...) while((s32[]{:T(128)}, f32[128,512]{1,0:T(8,128)S(1)}, ...), condition=%wide.region_4.5_spmd.clone, body=%wide.region_3.4_spmd.clone.sunk | while | flops 134914 | bytes 545401 | solution.py:45
  57.0 0.8 subtract_divide_fusion.2
  58.7 0.8 subtract_divide_fusion.2
  60.4 0.8 subtract_divide_fusion.2
  62.1 0.8 subtract_divide_fusion.2
  63.8 0.8 subtract_divide_fusion.2
  65.5 0.8 subtract_divide_fusion.2
  67.2 0.8 subtract_divide_fusion.2
  68.9 0.8 subtract_divide_fusion.2
  79.1 0.8 subtract_divide_fusion.2
  87.6 0.8 subtract_divide_fusion.2
  89.3 0.8 subtract_divide_fusion.2
  99.5 0.8 subtract_divide_fusion.2
  121.7 0.8 subtract_divide_fusion.2
  123.4 0.8 subtract_divide_fusion.2
  125.1 0.8 subtract_divide_fusion.2
  126.8 0.8 subtract_divide_fusion.2
  128.5 0.8 subtract_divide_fusion.2
  130.2 0.8 subtract_divide_fusion.2
  142.1 0.8 subtract_divide_fusion.2
  143.8 0.8 subtract_divide_fusion.2
  145.5 0.8 subtract_divide_fusion.2
  167.6 0.8 subtract_divide_fusion.2
  169.3 0.8 subtract_divide_fusion.2
  171.0 0.8 subtract_divide_fusion.2
  177.8 0.8 subtract_divide_fusion.2
  179.5 0.8 subtract_divide_fusion.2
  181.2 0.8 subtract_divide_fusion.2
  182.9 0.8 subtract_divide_fusion.2
  184.6 0.8 subtract_divide_fusion.2
  186.3 0.8 subtract_divide_fusion.2
  201.6 0.8 subtract_divide_fusion.2
  203.3 0.8 subtract_divide_fusion.2
  206.8 0.8 subtract_divide_fusion.2
  208.5 0.8 subtract_divide_fusion.2
  210.2 0.8 subtract_divide_fusion.2
  211.9 0.8 subtract_divide_fusion.2
  213.6 0.8 subtract_divide_fusion.2
  215.3 0.8 subtract_divide_fusion.2
  274.9 27.7 %multiply_convert_fusion = bf16[16384,1024]{1,0:T(8,128)(2,1)} fusion(bf16[512,16384]{1,0:T(8,128)(2,1)} %all-gather.4.cloned.1.call-done, bf16[512,1024]{1,0:T(8,128)(2,1)S(1)} %copy-done), kind=kOutput, calls=%fused_computation.6 | convolution fusion | flops 17213423616 | bytes 51380224 | tf_op jit(solution)/shard_map/dot_general | solution.py:63
  302.8 73.4 %all-reduce.3.cloned.1.call-done = bf16[128,512]{1,0:T(8,128)(2,1)} async-done(((bf16[128,512]{1,0:T(8,128)(2,1)}), bf16[128,512]{1,0:T(8,128)(2,1)}) %all-reduce.3.cloned.1.call-update) | async-done | bytes 131088 | tf_op jit(solution)/shard_map/psum | solution.py:22
  376.3 3.3 subtract_select_fusion
  379.6 41.1 %reduce-scatter.2.cloned.1.call-done = bf16[8192,1024]{1,0:T(8,128)(2,1)} async-done(((bf16[16384,1024]{1,0:T(8,128)(2,1)}), bf16[8192,1024]{1,0:T(8,128)(2,1)}) %reduce-scatter.2.cloned.1.call-update) | async-done | bytes 16777232 | tf_op jit(solution)/shard_map/reduce_scatter | solution.py:66
  420.7 18.6 %convert_element_type.23 = f32[8192,1024]{1,0:T(8,128)} convert(bf16[8192,1024]{1,0:T(8,128)(2,1)} %reduce-scatter.2.cloned.1.call-done) | non-fusion elementwise | flops 8388608 | bytes 50331648 | tf_op jit(solution)/shard_map/convert_element_type | solution.py:68
  (758 shorter events, 184.4 us)
Async XLA Ops:
  7.2 267.7 %all-gather.4.cloned.1.call-start = ((), (), s32[]{:S(2)}) async-start(), calls=%async_computation.1 | async-start | bytes 17825792 | tf_op jit(solution)/shard_map/all_gather | solution.py:62
  7.2 47.7 %copy-start.2 = (f32[128,1024]{1,0:T(8,128)S(1)}, f32[128,1024]{1,0:T(8,128)}, u32[]{:S(2)}) copy-start(f32[128,1024]{1,0:T(8,128)} %param.10) | copy-start | bytes 1572868
  8.8 46.1 %slice-start = ((f32[512,1024]{1,0:T(8,128)}), f32[512,128]{1,0:T(8,128)S(1)}, s32[]{:S(2)}) async-start(f32[512,1024]{1,0:T(8,128)} %param.9), calls=%async_computation.4 | async-start | bytes 524288 | tf_op jit(solution)/shard_map/slice | solution.py:71
  52.2 4.1 copy-start.3
  54.8 321.5 %all-reduce.3.cloned.1.call-start = ((), (), s32[]{:S(2)}) async-start(), calls=%async_computation.3 | async-start | bytes 262144 | tf_op jit(solution)/shard_map/psum | solution.py:22
  55.0 219.9 %copy-start = (bf16[512,1024]{1,0:T(8,128)(2,1)S(1)}, bf16[512,1024]{1,0:T(8,128)(2,1)}, u32[]{:S(2)}) copy-start(bf16[512,1024]{1,0:T(8,128)(2,1)} %fusion.4) | copy-start | bytes 3145732
  274.8 145.8 %reduce-scatter.2.cloned.1.call-start = ((), (), s32[]{:S(2)}) async-start(), calls=%async_computation.2 | async-start | bytes 50331648 | tf_op jit(solution)/shard_map/reduce_scatter | solution.py:66
  302.7 73.6 %copy-start.1 = (f32[512,1024]{1,0:T(8,128)S(1)}, f32[512,1024]{1,0:T(8,128)}, u32[]{:S(2)}) copy-start(f32[512,1024]{1,0:T(8,128)} %param.9) | copy-start | bytes 6291460
Sparse Core Ops, SparseCore 0:
  54.9 192.1 all-gather.3
  275.0 101.2 all-reduce.2
  379.1 41.4 reduce-scatter.1
